TPU v7x, 256 devices: a whole 4x4x8 slice. The times are simulated.
256 devices in a mesh: row: 16 (over z, core), col: 16 (over x, y).
Axes of the slice: x: 4, y: 4, z: 8, core: 2. Of those that a mesh axis runs over, the one named last changes fastest.
Arguments:
- f_blocks: bfloat16 [32768, 8192], P('row', 'col'), may hold values from -0.25 to 0.25
- block_cols: int32 [512, 128], P('row', 'col'), may hold values from 0 to 23, as said below
- block_counts: int32 [512, 16], P('row', 'col'), may hold values from 1 to 8, as said below
- p_matrix: bfloat16 [24576, 8192], P('row', 'col'), may hold values from -6 to 6
Outputs:
- product: bfloat16 [32768, 8192], P('row', 'col')
Inputs may be any that keep to these rules, and one draw needn't show every extreme that they name: `block_cols`: within one block row of one stored tile the 8 listed block columns are distinct, padded slots included. `block_counts`: some block row of every stored tile is full.
All inputs are finite; a program needn't handle non-finite values.
Results may differ from a plain program's by a relative error of at most 0.001.
Values may be sent and summed in bfloat16 or wider, within the bound.
A program may use at most 64 MiB of HBM per device.

v0:
```python
import jax
import jax.numpy as jnp
from jax import lax
from jax.sharding import PartitionSpec as P


def shifted(block, axis, distance):
    devices = range(lax.axis_size(axis))
    route = [((i - distance) % len(devices), i) for i in devices]
    return lax.ppermute(block, axis, route)


def expand_tile(strips, cols, live, depth, edge):
    nrows, slots = cols.shape
    places = lax.broadcasted_iota(jnp.int32, (nrows, slots, depth), 2)
    match = (cols[:, :, None] == places) & live[:, :, None]
    viewed = strips.reshape(nrows, edge, slots, 1, edge)
    spread = jnp.where(match[:, None, :, :, None], viewed, jnp.zeros((), strips.dtype))
    return jnp.sum(spread, axis=2).reshape(nrows * edge, depth * edge)


def body(f_blocks, block_cols, block_counts, p_matrix):
    nrows, slots = block_cols.shape
    edge = 64
    depth = p_matrix.shape[0] // edge
    live = lax.broadcasted_iota(jnp.int32, (nrows, slots), 1) < block_counts
    p_second = shifted(p_matrix, "row", -1)
    expanded = expand_tile(f_blocks, block_cols, live, depth, edge)
    following = shifted(expanded, "col", -1)
    total = jnp.dot(expanded, p_matrix, preferred_element_type=jnp.float32)
    total = total + jnp.dot(following, p_second, preferred_element_type=jnp.float32)
    return total.astype(jnp.bfloat16)


def solution(mesh):
    return jax.shard_map(
        body,
        mesh=mesh,
        in_specs=(P("row", "col"), P("row", "col"), P("row", "col"), P("row", "col")),
        out_specs=P("row", "col"),
        check_vma=False,
    )
```

profile of v0, /device:TPU:94, one launch (start us, length us, event | category | flops | bytes accessed | tf_op | source)
XLA Modules:
  0.0 222.3 jit_solution(4530114429508373037)
XLA Ops:
  0.0 0.0 copy-start
  0.0 0.0 copy-start.1
  0.0 6.2 %broadcast_in_dim.26 = bf16[32,64,8,64]{3,2,1,0:T(8,128)(2,1)} reshape(bf16[2048,512]{1,0:T(8,128)(2,1)} %param.4) | data formatting | bytes 4194304 | tf_op jit(solution)/shard_map/jit(_where)/broadcast_in_dim | solution.py:18
  6.2 0.0 copy-done
  6.2 0.1 copy.6
  6.3 0.0 copy-done.1
  6.3 0.1 iota_compare_fusion.1
  6.4 0.1 fusion
  6.5 53.5 %select_reduce_fusion = bf16[32,64,24,64]{3,2,1,0:T(8,128)(2,1)} fusion(pred[32,8,24]{2,1,0:T(8,128)(4,1)S(1)} %fusion, bf16[32,64,8,64]{3,2,1,0:T(8,128)(2,1)} %broadcast_in_dim.26), kind=kLoop, calls=%fused_computation | loop fusion | flops 47185920 | bytes 8394752 | tf_op jit(solution)/shard_map/reduce_sum | solution.py:19
  60.0 0.0 copy-start.2
  60.0 17.0 %reshape.31 = bf16[2048,1536]{1,0:T(8,128)(2,1)} reshape(bf16[32,64,24,64]{3,2,1,0:T(8,128)(2,1)} %select_reduce_fusion) | data formatting | bytes 12582912 | tf_op jit(solution)/shard_map/reshape | solution.py:19
  77.0 0.7 collective-permute-start
  77.7 0.0 copy-done.2
  77.7 0.0 collective-permute-start.1
  77.7 5.5 %fusion.1 = f32[2048,512]{1,0:T(8,128)S(1)} fusion(bf16[2048,1536]{1,0:T(8,128)(2,1)} %reshape.31, bf16[1536,512]{1,0:T(8,128)(2,1)S(1)} %copy-done.2), kind=kOutput, calls=%fused_computation.5 | convolution fusion | flops 3221225472 | bytes 12058624 | tf_op jit(solution)/shard_map/dot_general | solution.py:30
  83.2 12.4 %collective-permute-done.1 = bf16[1536,512]{1,0:T(8,128)(2,1)S(1)} collective-permute-done((bf16[1536,512]{1,0:T(8,128)(2,1)S(1)}, bf16[1536,512]{1,0:T(8,128)(2,1)S(1)}, u32[]{:S(2)}, u32[]{:S(2)}) %collective-permute-start.1) | collective-permute-done | bytes 1572896 | tf_op jit(solution)/shard_map/ppermute | solution.py:10
  95.7 122.1 %collective-permute-done = bf16[2048,1536]{1,0:T(8,128)(2,1)S(1)} collective-permute-done((bf16[2048,1536]{1,0:T(8,128)(2,1)}, bf16[2048,1536]{1,0:T(8,128)(2,1)S(1)}, u32[]{:S(2)}, u32[]{:S(2)}) %collective-permute-start) | collective-permute-done | bytes 6291488 | tf_op jit(solution)/shard_map/ppermute | solution.py:10
  217.8 4.5 %add_convert_fusion = bf16[2048,512]{1,0:T(8,128)(2,1)} fusion(f32[2048,512]{1,0:T(8,128)S(1)} %fusion.1, bf16[2048,1536]{1,0:T(8,128)(2,1)S(1)} %collective-permute-done, bf16[1536,512]{1,0:T(8,128)(2,1)S(1)} %collective-permute-done.1), kind=kOutput, calls=%fused_computation.1 | convolution fusion | flops 3223322624 | bytes 14155776 | tf_op jit(solution)/shard_map/dot_general | solution.py:31
Async XLA Ops:
  0.0 6.2 %copy-start = (s32[32,8]{0,1:T(8,128)S(1)}, s32[32,8]{0,1:T(8,128)}, u32[]{:S(2)}) copy-start(s32[32,8]{0,1:T(8,128)} %param.5) | copy-start | bytes 3076
  0.0 6.3 %copy-start.1 = (s32[32,1]{0,1:T(1,128)S(1)}, s32[32,1]{0,1:T(1,128)}, u32[]{:S(2)}) copy-start(s32[32,1]{0,1:T(1,128)} %param.6) | copy-start | bytes 388
  60.0 17.7 %copy-start.2 = (bf16[1536,512]{1,0:T(8,128)(2,1)S(1)}, bf16[1536,512]{1,0:T(8,128)(2,1)}, u32[]{:S(2)}) copy-start(bf16[1536,512]{1,0:T(8,128)(2,1)} %param.7) | copy-start | bytes 4718596
  77.0 140.8 %collective-permute-start = (bf16[2048,1536]{1,0:T(8,128)(2,1)}, bf16[2048,1536]{1,0:T(8,128)(2,1)S(1)}, u32[]{:S(2)}, u32[]{:S(2)}) collective-permute-start(bf16[2048,1536]{1,0:T(8,128)(2,1)} %reshape.31), channel_id=1, source_target_pairs={{1,0},{2,1},{3,2},{4,3},{5,4},{6,5},{7,6},{8,7},{9,8},{10,9},{11,1... | collective-permute-start | bytes 18874376 | tf_op jit(solution)/shard_map/ppermute | solution.py:10
  77.7 17.9 %collective-permute-start.1 = (bf16[1536,512]{1,0:T(8,128)(2,1)S(1)}, bf16[1536,512]{1,0:T(8,128)(2,1)S(1)}, u32[]{:S(2)}, u32[]{:S(2)}) collective-permute-start(bf16[1536,512]{1,0:T(8,128)(2,1)S(1)} %copy-done.2), channel_id=1, source_target_pairs={{16,0},{32,16},{48,32},{64,48},{80,64},{96,80},{112,96},{128,112},... | collective-permute-start | bytes 4718600 | tf_op jit(solution)/shard_map/ppermute | solution.py:10
where the time goes:
time: 223 us; the launch traced here: 222 us
  waiting for transfers between devices  135 us (61%)
  other arithmetic  53.7 us (24%)
  local copies, waits for them, and re-layouts  23.3 us (10%)
  matrix products  10 us (4%)
    ppermute x2, waiting for transfers between devices, shifted(): return lax.ppermute(block, axis, route)  135 us
    reduce_sum x1, other arithmetic, expand_tile(): return jnp.sum(spread, axis=2).reshape(nrows * edge, depth * edge)  53.5 us
    reshape x1, local copies, waits for them, and re-layouts, expand_tile(): return jnp.sum(spread, axis=2).reshape(nrows * edge, depth * edge)  17 us
    broadcast_in_dim x1, local copies, waits for them, and re-layouts, expand_tile(): jnp.where(match[:, None, :, :, None], viewed, jnp.zeros((), strips.dtype))  6.21 us
    dot_general x1, matrix products, body(): total = jnp.dot(expanded, p_matrix, preferred_element_type=jnp.float32)  5.5 us
    dot_general x1, matrix products, body(): jnp.dot(following, p_second, preferred_element_type=jnp.float32)  4.54 us
  transfers between devices with their start and end apart: 2, of which 2 were waited for; matrix products, arithmetic and copies ran while one was open for 2% of the time, Pallas kernels for 0%

commit v1 on v0

v1 whole, which is shorter than its diff:
```python
import functools

import jax
import jax.numpy as jnp
from jax import lax
from jax.experimental import pallas as pl
from jax.experimental.pallas import tpu as pltpu
from jax.sharding import PartitionSpec as P

EDGE = 64
CHUNK = 128
DIRECT = 12
RELAY = 4
P_STEP = 6
MESH = pl.DeviceIdType.MESH


def kernel(
    f_hbm, cols_h, cnt_h, p_hbm, out_hbm,
    cols_s, cnt_s, f_own, p_own, f_rx, hop1, hop2, p_rx, acc, outbuf,
    cols_rv, cnt_rv, cols_rs, cnt_rs,
    d_send, d_recv, r_send, r_recv, p_send, p_recv, m_send, m_recv, l_sem, o_sem,
):
    rows, width = f_hbm.shape
    slots = width // EDGE
    per = CHUNK // EDGE
    i = lax.axis_index("row")
    j = lax.axis_index("col")
    n_row = lax.axis_size("row")
    n_col = lax.axis_size("col")
    x, y = lax.div(j, 4), lax.rem(j, 4)
    to_direct = lax.rem(j + n_col - 1, n_col)
    from_direct = lax.rem(j + 1, n_col)
    to_ring = x * 4 + lax.rem(y + 1, 4)
    from_ring = x * 4 + lax.rem(y + 3, 4)
    nx = n_col // 4
    is3 = lax.div(y, 3)
    is2 = lax.div(y + 1, 3) - is3
    to_last = lax.rem(x + nx - is2, nx) * 4 + lax.rem(y + 1, 4)
    from_last = lax.rem(x + is3, nx) * 4 + lax.rem(y + 3, 4)
    to_p = lax.rem(i + n_row - 1, n_row)
    from_p = lax.rem(i + 1, n_row)

    own = [
        pltpu.make_async_copy(p_hbm, p_own, l_sem.at[0]),
        pltpu.make_async_copy(f_hbm, f_own, l_sem.at[1]),
        pltpu.make_async_copy(cols_h, cols_s, l_sem.at[4]),
        pltpu.make_async_copy(cnt_h, cnt_s, l_sem.at[5]),
    ]
    for copy in own:
        copy.start()

    barrier = pltpu.get_barrier_semaphore()
    for source in (from_direct, from_ring, from_last):
        pl.semaphore_signal(barrier, inc=1, device_id=(i, source), device_id_type=MESH)
    pl.semaphore_signal(barrier, inc=1, device_id=(from_p, j), device_id_type=MESH)
    pl.semaphore_wait(barrier, 4)

    def send(src, dst, ssem, rsem, target):
        return pltpu.make_async_remote_copy(
            src_ref=src, dst_ref=dst, send_sem=ssem, recv_sem=rsem,
            device_id=target, device_id_type=MESH,
        )

    meta = [
        send(cols_h, cols_rv, m_send.at[0], m_recv.at[0], (i, to_direct)),
        send(cnt_h, cnt_rv, m_send.at[1], m_recv.at[1], (i, to_direct)),
    ]
    p_copy = send(p_hbm, p_rx, p_send, p_recv, (to_p, j))
    direct = [
        send(f_hbm.at[pl.ds(k * CHUNK, CHUNK)], f_rx.at[pl.ds(k * CHUNK, CHUNK)],
             d_send.at[k], d_recv.at[k], (i, to_direct))
        for k in range(DIRECT)
    ]
    relay = []
    for k in range(3 * RELAY):
        hop, c = k // RELAY, k % RELAY
        part = pl.ds((DIRECT + c) * CHUNK, CHUNK)
        src = (f_hbm.at[part], hop1.at[c], hop2.at[c])[hop]
        dst = (hop1.at[c], hop2.at[c], f_rx.at[part])[hop]
        target = (to_ring, to_ring, to_last)[hop]
        relay.append(send(src, dst, r_send.at[k], r_recv.at[k], (i, target)))

    p_copy.start()
    for k in range(RELAY):
        direct[k].start()
        relay[k].start()
    for k in range(RELAY, DIRECT):
        direct[k].start()
    for copy in meta:
        copy.start()

    def term(f_ref, p_ref, cols, cnt, r):
        lhs = f_ref[pl.ds(pl.multiple_of(r * EDGE, EDGE), EDGE), :]
        lane = lax.broadcasted_iota(jnp.int32, lhs.shape, 1)
        lhs = jnp.where(lane < cnt[0, r] * EDGE, lhs, jnp.zeros_like(lhs))
        rhs = jnp.concatenate(
            [p_ref[cols[s, r]] for s in range(slots)],
            axis=0,
        )
        return jnp.dot(lhs, rhs, preferred_element_type=jnp.float32)

    for copy in own:
        copy.wait()

    @pl.loop(0, rows // EDGE)
    def _(r):
        acc[pl.ds(pl.multiple_of(r * EDGE, EDGE), EDGE), :] = term(f_own, p_own, cols_s, cnt_s, r)

    outs = {}

    def second(c):
        @pl.loop(c * per, (c + 1) * per)
        def _(r):
            part = pl.ds(pl.multiple_of(r * EDGE, EDGE), EDGE)
            total = acc[part, :] + term(f_rx, p_rx, cols_rs, cnt_rs, r)
            outbuf[part, :] = total.astype(outbuf.dtype)

        part = pl.ds(c * CHUNK, CHUNK)
        outs[c] = pltpu.make_async_copy(outbuf.at[part], out_hbm.at[part], o_sem.at[c])
        outs[c].start()

    done = 0
    for k in range(DIRECT):
        relay[k].wait_recv()
        if k < 2 * RELAY:
            relay[k + RELAY].start()
        direct[k].wait_recv()
        if k == P_STEP:
            for copy in meta:
                copy.wait()
            small = [
                pltpu.make_async_copy(cols_rv, cols_rs, l_sem.at[2]),
                pltpu.make_async_copy(cnt_rv, cnt_rs, l_sem.at[3]),
            ]
            for copy in small:
                copy.start()
            for copy in small:
                copy.wait()
            p_copy.wait()
        if k >= P_STEP:
            upto = k + 1 if k >= P_STEP + 2 else min(k + 1, done + 3)
            for c in range(done, upto):
                second(c)
            done = upto
            if k >= 2 * RELAY:
                second(DIRECT + k - 2 * RELAY)
    for copy in direct:
        copy.wait_send()
    for copy in relay:
        copy.wait_send()
    for copy in outs.values():
        copy.wait()


def body(f_blocks, block_cols, block_counts, p_matrix):
    rows, width = f_blocks.shape
    depth, wide = p_matrix.shape
    cols = block_cols.T
    counts = block_counts.T
    dma = pltpu.SemaphoreType.DMA
    any_spec = pl.BlockSpec(memory_space=pl.ANY)
    hbm = pl.BlockSpec(memory_space=pltpu.HBM)
    return pl.pallas_call(
        kernel,
        out_shape=jax.ShapeDtypeStruct((rows, wide), jnp.bfloat16),
        in_specs=[hbm, hbm, hbm, hbm],
        out_specs=any_spec,
        scratch_shapes=[
            pltpu.SMEM(cols.shape, jnp.int32),
            pltpu.SMEM(counts.shape, jnp.int32),
            pltpu.VMEM((rows, width), jnp.bfloat16),
            pltpu.VMEM((depth // EDGE, EDGE, wide), jnp.bfloat16),
            pltpu.VMEM((rows, width), jnp.bfloat16),
            pltpu.VMEM((RELAY, CHUNK, width), jnp.bfloat16),
            pltpu.VMEM((RELAY, CHUNK, width), jnp.bfloat16),
            pltpu.VMEM((depth // EDGE, EDGE, wide), jnp.bfloat16),
            pltpu.VMEM((rows, wide), jnp.float32),
            pltpu.VMEM((rows, wide), jnp.bfloat16),
            pltpu.VMEM(cols.shape, jnp.int32),
            pltpu.VMEM(counts.shape, jnp.int32),
            pltpu.SMEM(cols.shape, jnp.int32),
            pltpu.SMEM(counts.shape, jnp.int32),
            dma((DIRECT,)), dma((DIRECT,)),
            dma((3 * RELAY,)), dma((3 * RELAY,)),
            dma, dma,
            dma((2,)), dma((2,)),
            dma((6,)),
            dma((DIRECT + RELAY,)),
        ],
        compiler_params=pltpu.CompilerParams(
            collective_id=0, has_side_effects=True, vmem_limit_bytes=60000000
        ),
    )(f_blocks, cols, counts, p_matrix.reshape(depth // EDGE, EDGE, wide))


def solution(mesh):
    return jax.shard_map(
        body,
        mesh=mesh,
        in_specs=(P("row", "col"), P("row", "col"), P("row", "col"), P("row", "col")),
        out_specs=P("row", "col"),
        check_vma=False,
    )
```

time: 223 us -> 53 us (0.24)
  the two profiles are of different devices: /device:TPU:94 before, /device:TPU:102 now
where the time goes in v1:
time: 53 us; the launch traced here: 52.9 us
  Pallas kernels  49.8 us (94%)
  local copies, waits for them, and re-layouts  3.05 us (6%)
    pallas_call x1, Pallas kernels, body(): pl.pallas_call(kernel, out_shape=jax.ShapeDtypeStruct((rows, wide), jnp.b...  49.8 us
    unnamed x1, local copies, waits for them, and re-layouts  3.05 us

profile of v1, /device:TPU:102, one launch (start us, length us, event | category | flops | bytes accessed | tf_op | source)
XLA Modules:
  0.0 52.9 jit_solution(10257626941099673987)
XLA Ops:
  0.0 49.8 %shard_map.46 = bf16[2048,512]{1,0:T(8,128)(2,1)} custom-call(bf16[2048,512]{1,0:T(8,128)(2,1)} %f_hbm.1, s32[8,32]{1,0:T(8,128)} %bitcast.4, s32[1,32]{1,0:T(1,128)} %bitcast.5, bf16[24,64,512]{2,1,0:T(8,128)(2,1)} %bitcast.3), custom_call_target="tpu_custom_call" | custom-call | tf_op jit(solution)/shard_map/pallas_call | solution.py:164
  49.9 3.0 %copy.6 = bf16[2048,512]{1,0:T(8,128)(2,1)} copy(bf16[2048,512]{1,0:T(8,128)(2,1)} %shard_map.46) | data formatting | bytes 4194304

commit v2 on v1

v2 whole, which is shorter than its diff:
```python
import jax
import jax.numpy as jnp
from jax import lax
from jax.experimental import pallas as pl
from jax.experimental.pallas import tpu as pltpu
from jax.sharding import PartitionSpec as P

EDGE = 64
DIRECT = (128,) * 11 + (64, 64)
RELAY = (128, 128, 128, 64, 64)
P_TIME = 0.5
LAG = 0.12
SIDE = 4
MESH = pl.DeviceIdType.MESH


def starts(sizes, base=0):
    out = []
    for size in sizes:
        out.append(base)
        base += size
    return out


def kernel(
    f_hbm, cols_h, cnt_h, p_hbm, out_hbm,
    cols_s, cnt_s, f_own, p_own, f_rx, hop1, hop2, landed, p_rx, acc, out_ref,
    cols_rv, cnt_rv, cols_rs, cnt_rs,
    d_send, d_recv, r_send, r_recv, x_send, x_recv, p_send, p_recv, m_send, m_recv, l_sem, o_sem,
):
    rows, width = f_hbm.shape
    slots = width // EDGE
    split = sum(DIRECT)
    n_d, n_r = len(DIRECT), len(RELAY)
    d_at, r_at = starts(DIRECT), starts(RELAY)
    i = lax.axis_index("row")
    j = lax.axis_index("col")
    n_row = lax.axis_size("row")
    n_col = lax.axis_size("col")
    nx = n_col // SIDE
    x, y = lax.div(j, SIDE), lax.rem(j, SIDE)
    to_direct = lax.rem(j + n_col - 1, n_col)
    from_direct = lax.rem(j + 1, n_col)
    to_ring = x * SIDE + lax.rem(y + 1, SIDE)
    from_ring = x * SIDE + lax.rem(y + SIDE - 1, SIDE)
    to_x = lax.rem(x + nx - 1, nx) * SIDE + y
    from_x = lax.rem(x + 1, nx) * SIDE + y
    to_p = lax.rem(i + n_row - 1, n_row)
    from_p = lax.rem(i + 1, n_row)
    turn = lax.div(y + 1, SIDE - 1) - lax.div(y, SIDE - 1)

    own = [
        pltpu.make_async_copy(p_hbm, p_own, l_sem.at[0]),
        pltpu.make_async_copy(f_hbm, f_own, l_sem.at[1]),
        pltpu.make_async_copy(cols_h, cols_s, l_sem.at[4]),
        pltpu.make_async_copy(cnt_h, cnt_s, l_sem.at[5]),
    ]
    barrier = pltpu.get_barrier_semaphore()
    for source in (from_direct, from_ring, from_x):
        pl.semaphore_signal(barrier, inc=1, device_id=(i, source), device_id_type=MESH)
    pl.semaphore_signal(barrier, inc=1, device_id=(from_p, j), device_id_type=MESH)
    for copy in own:
        copy.start()
    pl.semaphore_wait(barrier, 4)

    def send(src, dst, ssem, rsem, target):
        return pltpu.make_async_remote_copy(
            src_ref=src, dst_ref=dst, send_sem=ssem, recv_sem=rsem,
            device_id=target, device_id_type=MESH,
        )

    meta = [
        send(cols_h, cols_rv, m_send.at[0], m_recv.at[0], (i, to_direct)),
        send(cnt_h, cnt_rv, m_send.at[1], m_recv.at[1], (i, to_direct)),
    ]
    p_copy = send(p_hbm, p_rx, p_send, p_recv, (to_p, j))
    direct = [
        send(f_hbm.at[pl.ds(at, size)], f_rx.at[pl.ds(at, size)],
             d_send.at[k], d_recv.at[k], (i, to_direct))
        for k, (at, size) in enumerate(zip(d_at, DIRECT))
    ]
    relay = []
    for hop in range(3):
        for k, (at, size) in enumerate(zip(r_at, RELAY)):
            part = pl.ds(at, size)
            src = (f_hbm.at[pl.ds(split + at, size)], hop1.at[part], hop2.at[turn, part])[hop]
            dst = (hop1.at[part], hop2.at[0, part], landed.at[part])[hop]
            e = hop * n_r + k
            relay.append(send(src, dst, r_send.at[e], r_recv.at[e], (i, to_ring)))
    cross = [
        send(hop2.at[0, pl.ds(at, size)], hop2.at[1, pl.ds(at, size)],
             x_send.at[k], x_recv.at[k], (i, to_x))
        for k, (at, size) in enumerate(zip(r_at, RELAY))
    ]

    for copy in meta:
        copy.start()
    for k in range(n_d):
        direct[k].start()
        if k < n_r:
            relay[k].start()
        if k == 0:
            p_copy.start()
    def term(lhs, p_ref, cols, cnt, r):
        lane = lax.broadcasted_iota(jnp.int32, lhs.shape, 1)
        lhs = jnp.where(lane < cnt[0, r] * EDGE, lhs, jnp.zeros_like(lhs))
        rhs = jnp.concatenate([p_ref[cols[s, r]] for s in range(slots)], axis=0)
        return jnp.dot(lhs, rhs, preferred_element_type=jnp.float32)

    def span(r):
        return pl.ds(pl.multiple_of(r * EDGE, EDGE), EDGE)

    for copy in own:
        copy.wait()

    @pl.loop(0, rows // EDGE)
    def _(r):
        acc[span(r), :] = term(f_own[span(r), :], p_own, cols_s, cnt_s, r)

    first_late = split // EDGE

    outs = []

    def put(lo, hi):
        part = pl.ds(lo * EDGE, (hi - lo) * EDGE)
        outs.append(pltpu.make_async_copy(out_ref.at[part], out_hbm.at[part], o_sem.at[lo]))
        outs[-1].start()

    def second_direct(lo, hi):
        @pl.loop(lo, hi)
        def _(r):
            total = acc[span(r), :] + term(f_rx[span(r), :], p_rx, cols_rs, cnt_rs, r)
            out_ref[span(r), :] = total.astype(out_ref.dtype)

        put(lo, hi)

    def second_late(lo, hi):
        @pl.loop(lo, hi)
        def _(r):
            lhs = landed[span(r - first_late), :]
            total = acc[span(r), :] + term(lhs, p_rx, cols_rs, cnt_rs, r)
            out_ref[span(r), :] = total.astype(out_ref.dtype)

        put(lo, hi)

    events = [((at + size) / split, 1, k) for k, (at, size) in enumerate(zip(d_at, DIRECT))]
    events += [
        ((hop * (rows - split) + at + size) / split, 0, hop * n_r + k)
        for hop in range(3) for k, (at, size) in enumerate(zip(r_at, RELAY))
    ]
    events += [
        ((rows - split + at + size) / split + LAG, 2, k)
        for k, (at, size) in enumerate(zip(r_at, RELAY))
    ]
    done = ready = 0
    late = []
    have_p = False
    for time, kind, k in sorted(events):
        if kind == 1:
            direct[k].wait_recv()
            ready = (d_at[k] + DIRECT[k]) // EDGE
        elif kind == 2:

            @pl.when(turn == 1)
            def _():
                cross[k].wait_recv()

            relay[2 * n_r + k].start()
        else:
            relay[k].wait_recv()
            if k < n_r:
                relay[k + n_r].start()
            elif k < 2 * n_r:

                @pl.when(turn == 1)
                def _():
                    cross[k - n_r].start()
            else:
                late.append(k - 2 * n_r)
        if time >= P_TIME and not have_p:
            have_p = True
            for copy in meta:
                copy.wait()
            small = [
                pltpu.make_async_copy(cols_rv, cols_rs, l_sem.at[2]),
                pltpu.make_async_copy(cnt_rv, cnt_rs, l_sem.at[3]),
            ]
            for copy in small:
                copy.start()
            for copy in small:
                copy.wait()
            p_copy.wait()
        if have_p and kind == 1:
            upto = min(ready, done + 6)
            second_direct(done, upto)
            done = upto
            while late:
                c = late.pop(0)
                lo = (split + r_at[c]) // EDGE
                second_late(lo, lo + RELAY[c] // EDGE)
    if done < ready:
        second_direct(done, ready)
    for c in late:
        lo = (split + r_at[c]) // EDGE
        second_late(lo, lo + RELAY[c] // EDGE)
    for copy in direct + relay:
        copy.wait_send()

    @pl.when(turn == 1)
    def _():
        for copy in cross:
            copy.wait_send()

    for copy in outs:
        copy.wait()


def body(f_blocks, block_cols, block_counts, p_matrix):
    rows, width = f_blocks.shape
    depth, wide = p_matrix.shape
    cols = block_cols.T
    counts = block_counts.T
    tiles = (depth // EDGE, EDGE, wide)
    late = sum(RELAY)
    dma = pltpu.SemaphoreType.DMA
    any_spec = pl.BlockSpec(memory_space=pl.ANY)
    return pl.pallas_call(
        kernel,
        out_shape=jax.ShapeDtypeStruct((rows, wide), jnp.bfloat16),
        in_specs=[any_spec] * 4,
        out_specs=any_spec,
        scratch_shapes=[
            pltpu.SMEM(cols.shape, jnp.int32),
            pltpu.SMEM(counts.shape, jnp.int32),
            pltpu.VMEM((rows, width), jnp.bfloat16),
            pltpu.VMEM(tiles, jnp.bfloat16),
            pltpu.VMEM((sum(DIRECT), width), jnp.bfloat16),
            pltpu.VMEM((late, width), jnp.bfloat16),
            pltpu.VMEM((2, late, width), jnp.bfloat16),
            pltpu.VMEM((late, width), jnp.bfloat16),
            pltpu.VMEM(tiles, jnp.bfloat16),
            pltpu.VMEM((rows, wide), jnp.float32),
            pltpu.VMEM((rows, wide), jnp.bfloat16),
            pltpu.VMEM(cols.shape, jnp.int32),
            pltpu.VMEM(counts.shape, jnp.int32),
            pltpu.SMEM(cols.shape, jnp.int32),
            pltpu.SMEM(counts.shape, jnp.int32),
            dma((len(DIRECT),)), dma((len(DIRECT),)),
            dma((3 * len(RELAY),)), dma((3 * len(RELAY),)),
            dma((len(RELAY),)), dma((len(RELAY),)),
            dma, dma,
            dma((2,)), dma((2,)),
            dma((6,)),
            dma((rows // EDGE,)),
        ],
        compiler_params=pltpu.CompilerParams(
            collective_id=0, has_side_effects=True, vmem_limit_bytes=63000000
        ),
    )(f_blocks, cols, counts, p_matrix.reshape(tiles))


def solution(mesh):
    return jax.shard_map(
        body,
        mesh=mesh,
        in_specs=(P("row", "col"), P("row", "col"), P("row", "col"), P("row", "col")),
        out_specs=P("row", "col"),
        check_vma=False,
    )
```

time: 53 us -> 45.2 us (0.85)
  the two profiles are of different devices: /device:TPU:102 before, /device:TPU:94 now
where the time goes in v2:
time: 45.2 us; the launch traced here: 44.7 us
  Pallas kernels  41.7 us (92%)
  local copies, waits for them, and re-layouts  3.05 us (7%)
    pallas_call x1, Pallas kernels, body(): pl.pallas_call(kernel, out_shape=jax.ShapeDtypeStruct((rows, wide), jnp.b...  41.7 us
    unnamed x1, local copies, waits for them, and re-layouts  3.05 us

profile of v2, /device:TPU:94, one launch (start us, length us, event | category | flops | bytes accessed | tf_op | source)
XLA Modules:
  0.0 44.7 jit_solution(11220788916047420839)
XLA Ops:
  0.0 41.7 %shard_map.46 = bf16[2048,512]{1,0:T(8,128)(2,1)} custom-call(bf16[2048,512]{1,0:T(8,128)(2,1)} %f_hbm.1, s32[8,32]{1,0:T(8,128)} %bitcast.4, s32[1,32]{1,0:T(1,128)} %bitcast.5, bf16[24,64,512]{2,1,0:T(8,128)(2,1)} %bitcast.3), custom_call_target="tpu_custom_call" | custom-call | tf_op jit(solution)/shard_map/pallas_call | solution.py:227
  41.7 3.0 %copy.6 = bf16[2048,512]{1,0:T(8,128)(2,1)} copy(bf16[2048,512]{1,0:T(8,128)(2,1)} %shard_map.46) | data formatting | bytes 4194304

commit v3 on v2

--- a/solution.py
+++ b/solution.py
@@ -23,10 +23,10 @@
 
 
 def kernel(
-    f_hbm, cols_h, cnt_h, p_hbm, out_hbm,
-    cols_s, cnt_s, f_own, p_own, f_rx, hop1, hop2, landed, p_rx, acc, out_ref,
+    f_hbm, cols_h, cnt_h, p_hbm, out_ref,
+    cols_s, cnt_s, f_own, p_own, f_rx, hop1, hop2, landed, p_rx, acc,
     cols_rv, cnt_rv, cols_rs, cnt_rs,
-    d_send, d_recv, r_send, r_recv, x_send, x_recv, p_send, p_recv, m_send, m_recv, l_sem, o_sem,
+    d_send, d_recv, r_send, r_recv, x_send, x_recv, p_send, p_recv, m_send, m_recv, l_sem,
 ):
     rows, width = f_hbm.shape
     slots = width // EDGE
@@ -119,20 +119,11 @@
 
     first_late = split // EDGE
 
-    outs = []
-
-    def put(lo, hi):
-        part = pl.ds(lo * EDGE, (hi - lo) * EDGE)
-        outs.append(pltpu.make_async_copy(out_ref.at[part], out_hbm.at[part], o_sem.at[lo]))
-        outs[-1].start()
-
     def second_direct(lo, hi):
         @pl.loop(lo, hi)
         def _(r):
             total = acc[span(r), :] + term(f_rx[span(r), :], p_rx, cols_rs, cnt_rs, r)
             out_ref[span(r), :] = total.astype(out_ref.dtype)
-
-        put(lo, hi)
 
     def second_late(lo, hi):
         @pl.loop(lo, hi)
@@ -140,8 +131,6 @@
             lhs = landed[span(r - first_late), :]
             total = acc[span(r), :] + term(lhs, p_rx, cols_rs, cnt_rs, r)
             out_ref[span(r), :] = total.astype(out_ref.dtype)
-
-        put(lo, hi)
 
     events = [((at + size) / split, 1, k) for k, (at, size) in enumerate(zip(d_at, DIRECT))]
     events += [
@@ -211,9 +200,6 @@
         for copy in cross:
             copy.wait_send()
 
-    for copy in outs:
-        copy.wait()
-
 
 def body(f_blocks, block_cols, block_counts, p_matrix):
     rows, width = f_blocks.shape
@@ -226,9 +212,9 @@
     any_spec = pl.BlockSpec(memory_space=pl.ANY)
     return pl.pallas_call(
         kernel,
-        out_shape=jax.ShapeDtypeStruct((rows, wide), jnp.bfloat16),
+        out_shape=pltpu.VMEM((rows, wide), jnp.bfloat16),
         in_specs=[any_spec] * 4,
-        out_specs=any_spec,
+        out_specs=pl.BlockSpec(memory_space=pltpu.VMEM),
         scratch_shapes=[
             pltpu.SMEM(cols.shape, jnp.int32),
             pltpu.SMEM(counts.shape, jnp.int32),
@@ -240,7 +226,6 @@
             pltpu.VMEM((late, width), jnp.bfloat16),
             pltpu.VMEM(tiles, jnp.bfloat16),
             pltpu.VMEM((rows, wide), jnp.float32),
-            pltpu.VMEM((rows, wide), jnp.bfloat16),
             pltpu.VMEM(cols.shape, jnp.int32),
             pltpu.VMEM(counts.shape, jnp.int32),
             pltpu.SMEM(cols.shape, jnp.int32),
@@ -251,12 +236,11 @@
             dma, dma,
             dma((2,)), dma((2,)),
             dma((6,)),
-            dma((rows // EDGE,)),
         ],
         compiler_params=pltpu.CompilerParams(
             collective_id=0, has_side_effects=True, vmem_limit_bytes=63000000
         ),
-    )(f_blocks, cols, counts, p_matrix.reshape(tiles))
+    )(*(pltpu.with_memory_space_constraint(a, pltpu.HBM) for a in (f_blocks, cols, counts, p_matrix.reshape(tiles))))
 
 
 def solution(mesh):

time: 45.2 us -> 42.6 us (0.942)
  local copies, waits for them, and re-layouts: 3.05 us -> 1.32 us
  Pallas kernels: 41.7 us -> 40.8 us
    unnamed x1, local copies, waits for them, and re-layouts: 3.05 us -> 1.32 us
    pallas_call x1, Pallas kernels: 41.7 us -> 40.8 us  [body(): pl.pallas_call(kernel, out_shape=pltpu.VMEM((rows, wide), jnp.bfloat16),...]
where the time goes in v3:
time: 42.6 us; the launch traced here: 42.1 us
  Pallas kernels  40.8 us (96%)
  local copies, waits for them, and re-layouts  1.32 us (3%)
    pallas_call x1, Pallas kernels, body(): pl.pallas_call(kernel, out_shape=pltpu.VMEM((rows, wide), jnp.bfloat16),...  40.8 us
    unnamed x1, local copies, waits for them, and re-layouts  1.32 us

profile of v3, /device:TPU:94, one launch (start us, length us, event | category | flops | bytes accessed | tf_op | source)
XLA Modules:
  0.0 42.1 jit_solution(8188502136406838843)
XLA Ops:
  0.0 40.8 %shard_map.46 = bf16[2048,512]{1,0:T(8,128)(2,1)S(1)} custom-call(bf16[2048,512]{1,0:T(8,128)(2,1)} %f_hbm.1, s32[8,32]{1,0:T(8,128)} %bitcast.4, s32[1,32]{1,0:T(1,128)} %bitcast.5, bf16[24,64,512]{2,1,0:T(8,128)(2,1)} %bitcast.3), custom_call_target="tpu_custom_call" | custom-call | tf_op jit(solution)/shard_map/pallas_call | solution.py:213
  40.8 1.3 %copy.6 = bf16[2048,512]{1,0:T(8,128)(2,1)} copy(bf16[2048,512]{1,0:T(8,128)(2,1)S(1)} %shard_map.46) | data formatting | bytes 4194304

commit v4 on v3

--- a/solution.py
+++ b/solution.py
@@ -8,8 +8,10 @@
 EDGE = 64
 DIRECT = (128,) * 11 + (64, 64)
 RELAY = (128, 128, 128, 64, 64)
-P_TIME = 0.5
+EXTRA = DIRECT[-1]
+P_TIME = 0.55
 LAG = 0.12
+SHIFT = 0.2
 SIDE = 4
 MESH = pl.DeviceIdType.MESH
 
@@ -26,7 +28,7 @@
     f_hbm, cols_h, cnt_h, p_hbm, out_ref,
     cols_s, cnt_s, f_own, p_own, f_rx, hop1, hop2, landed, p_rx, acc,
     cols_rv, cnt_rv, cols_rs, cnt_rs,
-    d_send, d_recv, r_send, r_recv, x_send, x_recv, p_send, p_recv, m_send, m_recv, l_sem,
+    d_send, d_recv, r_send, r_recv, x_send, x_recv, p_send, p_recv, m_send, m_recv, l_sem, ready,
 ):
     rows, width = f_hbm.shape
     slots = width // EDGE
@@ -56,12 +58,45 @@
         pltpu.make_async_copy(cnt_h, cnt_s, l_sem.at[5]),
     ]
     barrier = pltpu.get_barrier_semaphore()
-    for source in (from_direct, from_ring, from_x):
-        pl.semaphore_signal(barrier, inc=1, device_id=(i, source), device_id_type=MESH)
-    pl.semaphore_signal(barrier, inc=1, device_id=(from_p, j), device_id_type=MESH)
+
+    def tell(when, sem, device):
+        @pl.when(when)
+        def _():
+            pl.semaphore_signal(sem, inc=1, device_id=device, device_id_type=MESH)
+
+    def after(when, sem):
+        @pl.when(when)
+        def _():
+            pl.semaphore_wait(sem, 1)
+
+    first_i, last_i = i == 0, i == n_row - 1
+    first_y, last_y = y == 0, y == SIDE - 1
+    turns = turn == 1
+    first_x = jnp.logical_and(turns, x == 0)
+    last_x = jnp.logical_and(turns, x == nx - 1)
+    tell(jnp.logical_not(last_y), barrier, (i, to_ring))
+    tell(first_y, barrier, (i, from_ring))
+    tell(jnp.logical_not(last_y), barrier, (i, from_direct))
+    tell(first_y, barrier, (i, to_direct))
+    tell(jnp.logical_not(last_i), barrier, (from_p, j))
+    tell(first_i, barrier, (to_p, j))
+    tell(jnp.logical_and(turns, x != nx - 1), barrier, (i, from_x))
+    tell(first_x, barrier, (i, to_x))
+    tell(jnp.logical_and(i == 1, first_y), barrier, (to_p, j))
     for copy in own:
         copy.start()
-    pl.semaphore_wait(barrier, 4)
+    inner_y = 1 - lax.div(SIDE - 1 - y, SIDE - 1)
+    edge_y = lax.div(y, SIDE - 1)
+    inner_i = 1 - lax.div(n_row - 1 - i, n_row - 1)
+    inner_x = 1 - lax.div(nx - 1 - x, nx - 1)
+    expected = inner_i + lax.div(i, n_row - 1) + 2 * inner_y + 2 * edge_y
+    expected = expected + turn * (inner_x + lax.div(x, nx - 1))
+    expected = expected + (1 - inner_i) * (1 - inner_y)
+    pl.semaphore_wait(barrier, expected)
+    tell(jnp.logical_not(first_y), ready.at[0], (i, from_ring))
+    tell(last_y, ready.at[1], (i, from_direct))
+    tell(last_i, ready.at[2], (from_p, j))
+    tell(last_x, ready.at[3], (i, from_x))
 
     def send(src, dst, ssem, rsem, target):
         return pltpu.make_async_remote_copy(
@@ -79,28 +114,54 @@
              d_send.at[k], d_recv.at[k], (i, to_direct))
         for k, (at, size) in enumerate(zip(d_at, DIRECT))
     ]
+    late_rows = sum(RELAY)
+    parts = [(late_rows, EXTRA, d_at[-1])]
+    parts += [(at, size, split + at) for at, size in zip(r_at, RELAY)]
+    n_c = len(parts)
+
+    def only(when, act):
+        if when is None:
+            act()
+        else:
+            pl.when(when)(act)
+
+    def sender_of(e):
+        return y == e // n_c if e % n_c == 0 else None
+
+    def receiver_of(e):
+        return y == e // n_c + 1 if e % n_c == 0 else None
+
     relay = []
     for hop in range(3):
-        for k, (at, size) in enumerate(zip(r_at, RELAY)):
+        for k, (at, size, row) in enumerate(parts):
             part = pl.ds(at, size)
-            src = (f_hbm.at[pl.ds(split + at, size)], hop1.at[part], hop2.at[turn, part])[hop]
-            dst = (hop1.at[part], hop2.at[0, part], landed.at[part])[hop]
-            e = hop * n_r + k
+            src = (f_hbm.at[pl.ds(row, size)], hop1.at[part], hop2.at[turn, part])[hop]
+            final = f_rx.at[pl.ds(row, size)] if k == 0 else landed.at[part]
+            dst = (hop1.at[part], hop2.at[0, part], final)[hop]
+            e = hop * n_c + k
             relay.append(send(src, dst, r_send.at[e], r_recv.at[e], (i, to_ring)))
     cross = [
         send(hop2.at[0, pl.ds(at, size)], hop2.at[1, pl.ds(at, size)],
              x_send.at[k], x_recv.at[k], (i, to_x))
-        for k, (at, size) in enumerate(zip(r_at, RELAY))
+        for k, (at, size, row) in enumerate(parts)
     ]
 
-    for copy in meta:
-        copy.start()
-    for k in range(n_d):
-        direct[k].start()
-        if k < n_r:
-            relay[k].start()
-        if k == 0:
-            p_copy.start()
+    def start_direct():
+        for copy in meta + direct[:-1]:
+            copy.start()
+
+    pl.when(jnp.logical_not(first_y))(start_direct)
+    pl.when(jnp.logical_not(first_y))(direct[-1].start)
+    pl.when(jnp.logical_not(first_i))(p_copy.start)
+    after(jnp.logical_not(last_y), ready.at[0])
+    for k in range(n_c):
+        only(sender_of(k), relay[k].start)
+    after(first_y, ready.at[1])
+    pl.when(first_y)(start_direct)
+    after(first_i, ready.at[2])
+    pl.when(first_i)(p_copy.start)
+    after(first_x, ready.at[3])
+
     def term(lhs, p_ref, cols, cnt, r):
         lane = lax.broadcasted_iota(jnp.int32, lhs.shape, 1)
         lhs = jnp.where(lane < cnt[0, r] * EDGE, lhs, jnp.zeros_like(lhs))
@@ -132,40 +193,39 @@
             total = acc[span(r), :] + term(lhs, p_rx, cols_rs, cnt_rs, r)
             out_ref[span(r), :] = total.astype(out_ref.dtype)
 
-    events = [((at + size) / split, 1, k) for k, (at, size) in enumerate(zip(d_at, DIRECT))]
-    events += [
-        ((hop * (rows - split) + at + size) / split, 0, hop * n_r + k)
-        for hop in range(3) for k, (at, size) in enumerate(zip(r_at, RELAY))
-    ]
-    events += [
-        ((rows - split + at + size) / split + LAG, 2, k)
-        for k, (at, size) in enumerate(zip(r_at, RELAY))
-    ]
-    done = ready = 0
+    events = []
+    for k, (at, size) in enumerate(zip(d_at, DIRECT)):
+        share = (at + size) / split
+        events.append((share + SHIFT * (1 - share), 1, k))
+    for k, (at, size, row) in enumerate(parts):
+        end = (size if k == 0 else at + size) / split
+        for hop in range(3):
+            events.append((hop * late_rows / split + end, 0, hop * n_c + k))
+        events.append((late_rows / split + end + LAG, 2, k))
+    done = fresh = 0
     late = []
     have_p = False
     for time, kind, k in sorted(events):
         if kind == 1:
-            direct[k].wait_recv()
-            ready = (d_at[k] + DIRECT[k]) // EDGE
+            only(None if k < n_d - 1 else jnp.logical_not(last_y), direct[k].wait_recv)
+            fresh = (d_at[k] + DIRECT[k]) // EDGE
         elif kind == 2:
-
-            @pl.when(turn == 1)
-            def _():
-                cross[k].wait_recv()
-
-            relay[2 * n_r + k].start()
+            pl.when(turns)(cross[k].wait_recv)
+            only(sender_of(2 * n_c + k), relay[2 * n_c + k].start)
+        elif k < 2 * n_c:
+
+            def forward():
+                relay[k].wait_recv()
+                if k < n_c:
+                    relay[k + n_c].start()
+                else:
+                    pl.when(turns)(cross[k - n_c].start)
+
+            only(receiver_of(k), forward)
         else:
-            relay[k].wait_recv()
-            if k < n_r:
-                relay[k + n_r].start()
-            elif k < 2 * n_r:
-
-                @pl.when(turn == 1)
-                def _():
-                    cross[k - n_r].start()
-            else:
-                late.append(k - 2 * n_r)
+            only(receiver_of(k), relay[k].wait_recv)
+            if k > 2 * n_c:
+                late.append(k - 2 * n_c - 1)
         if time >= P_TIME and not have_p:
             have_p = True
             for copy in meta:
@@ -180,20 +240,23 @@
                 copy.wait()
             p_copy.wait()
         if have_p and kind == 1:
-            upto = min(ready, done + 6)
+            upto = min(fresh, done + 6)
             second_direct(done, upto)
             done = upto
             while late:
                 c = late.pop(0)
                 lo = (split + r_at[c]) // EDGE
                 second_late(lo, lo + RELAY[c] // EDGE)
-    if done < ready:
-        second_direct(done, ready)
+    if done < fresh:
+        second_direct(done, fresh)
     for c in late:
         lo = (split + r_at[c]) // EDGE
         second_late(lo, lo + RELAY[c] // EDGE)
-    for copy in direct + relay:
+    for copy in direct[:-1]:
         copy.wait_send()
+    pl.when(jnp.logical_not(first_y))(direct[-1].wait_send)
+    for e in range(3 * n_c):
+        only(sender_of(e), relay[e].wait_send)
 
     @pl.when(turn == 1)
     def _():
@@ -208,6 +271,8 @@
     counts = block_counts.T
     tiles = (depth // EDGE, EDGE, wide)
     late = sum(RELAY)
+    held = late + EXTRA
+    n_c = len(RELAY) + 1
     dma = pltpu.SemaphoreType.DMA
     any_spec = pl.BlockSpec(memory_space=pl.ANY)
     return pl.pallas_call(
@@ -221,8 +286,8 @@
             pltpu.VMEM((rows, width), jnp.bfloat16),
             pltpu.VMEM(tiles, jnp.bfloat16),
             pltpu.VMEM((sum(DIRECT), width), jnp.bfloat16),
-            pltpu.VMEM((late, width), jnp.bfloat16),
-            pltpu.VMEM((2, late, width), jnp.bfloat16),
+            pltpu.VMEM((held, width), jnp.bfloat16),
+            pltpu.VMEM((2, held, width), jnp.bfloat16),
             pltpu.VMEM((late, width), jnp.bfloat16),
             pltpu.VMEM(tiles, jnp.bfloat16),
             pltpu.VMEM((rows, wide), jnp.float32),
@@ -231,11 +296,12 @@
             pltpu.SMEM(cols.shape, jnp.int32),
             pltpu.SMEM(counts.shape, jnp.int32),
             dma((len(DIRECT),)), dma((len(DIRECT),)),
-            dma((3 * len(RELAY),)), dma((3 * len(RELAY),)),
-            dma((len(RELAY),)), dma((len(RELAY),)),
+            dma((3 * n_c,)), dma((3 * n_c,)),
+            dma((n_c,)), dma((n_c,)),
             dma, dma,
             dma((2,)), dma((2,)),
             dma((6,)),
+            pltpu.SemaphoreType.REGULAR((4,)),
         ],
         compiler_params=pltpu.CompilerParams(
             collective_id=0, has_side_effects=True, vmem_limit_bytes=63000000

time: 42.6 us -> 42 us (0.986)
  no operation moved by 1% of the time
where the time goes in v4:
time: 42 us
  Pallas kernels  40.6 us (97%)
  local copies, waits for them, and re-layouts  1.32 us (3%)
    pallas_call x1, Pallas kernels, body(): pl.pallas_call(kernel, out_shape=pltpu.VMEM((rows, wide), jnp.bfloat16),...  40.6 us
    unnamed x1, local copies, waits for them, and re-layouts  1.32 us

profile of v4, /device:TPU:94, one launch (start us, length us, event | category | flops | bytes accessed | tf_op | source)
XLA Modules:
  0.0 42.0 jit_solution(3052107747832851745)
XLA Ops:
  0.0 40.6 %shard_map.46 = bf16[2048,512]{1,0:T(8,128)(2,1)S(1)} custom-call(bf16[2048,512]{1,0:T(8,128)(2,1)} %f_hbm.1, s32[8,32]{1,0:T(8,128)} %bitcast.4, s32[1,32]{1,0:T(1,128)} %bitcast.5, bf16[24,64,512]{2,1,0:T(8,128)(2,1)} %bitcast.3), custom_call_target="tpu_custom_call" | custom-call | tf_op jit(solution)/shard_map/pallas_call | solution.py:278
  40.6 1.3 %copy.6 = bf16[2048,512]{1,0:T(8,128)(2,1)} copy(bf16[2048,512]{1,0:T(8,128)(2,1)S(1)} %shard_map.46) | data formatting | bytes 4194304
